TPU v7x, 256 devices: a whole 4x4x8 slice. The times are simulated.
256 devices in a mesh: layer: 4 (over y), row: 8 (over x, core), col: 8 (over z).
Axes of the slice: x: 4, y: 4, z: 8, core: 2. Of those that a mesh axis runs over, the one named last changes fastest.
Arguments:
- l_blocks: bfloat16 [4, 64, 256, 256], P('layer', ('row', 'col')), may hold values from -3 to 3
- l_ids: int32 [4, 64], P('layer'), may hold values from 0 to 127, as said below
- u_blocks: bfloat16 [4, 64, 256, 256], P('layer', ('row', 'col')), may hold values from -3 to 3
- u_ids: int32 [4, 64], P('layer'), may hold values from 0 to 127, as said below
- inv_upper: bfloat16 [8, 256, 256], replicated, as said below
- inv_lower: bfloat16 [8, 256, 256], replicated, as said below
- row_order: int32 [16], replicated, may hold values from 0 to 15, as said below
- col_order: int32 [16], replicated, may hold values from 0 to 15, as said below
- front_in: float32 [16, 16, 256, 256], P('row', 'col', 'layer'), may hold values from -6 to 6
- leaf_lower: bfloat16 [256, 1024, 1024], P(('layer', 'row', 'col')), may hold values from -6 to 6
- leaf_upper: bfloat16 [256, 1024, 1024], P(('layer', 'row', 'col')), may hold values from -0.1875 to 0.1875
- leaf_front: bfloat16 [256, 1024, 1024], P(('layer', 'row', 'col')), may hold values from -6 to 6
Outputs:
- front_out: float32 [16, 16, 256, 256], P('row', 'col', 'layer')
- leaf_out: bfloat16 [256, 1024, 1024], P(('layer', 'row', 'col'))
Inputs may be any that keep to these rules, and one draw needn't show every extreme that they name: `l_ids`: within a layer the ids are distinct; the entry at index r * 8 + c has i = row_order[r * 2 + p] for some p < 2. `u_ids`: within a layer the ids are distinct; the entry at index r * 8 + c has j = col_order[c * 2 + q] for some q < 2. `row_order`: A permutation of the tile rows. `col_order`: A permutation of the tile columns. `inv_upper`: each block is upper triangular with a positive diagonal. `inv_lower`: each block is lower triangular with a positive diagonal.
All inputs are finite; a program needn't handle non-finite values.
Results may differ from a plain program's by a relative error of at most 0.0095.
Values may be sent and summed in bfloat16 or wider, within the bound.
No kernel may reach another device: no remote copies, remote signals or barrier semaphores. Data moves between devices by JAX's collectives and lax.ppermute only.
A program may use at most 128 MiB of HBM per device.

v0:
```python
import jax
import jax.numpy as jnp
from jax import lax
from jax.sharding import PartitionSpec as P


def place_all(carry, blocks, ids, wanted):
    matches = wanted[:, :, None] == ids[None, None, :]
    present = jnp.any(matches, axis=2)
    position = jnp.argmax(matches.astype(jnp.int32), axis=2)
    picked = blocks[position]
    return jnp.where(present[:, :, None, None], picked, carry)


def shards(
    l_blocks,
    l_ids,
    u_blocks,
    u_ids,
    inv_upper,
    inv_lower,
    row_order,
    col_order,
    front_in,
    leaf_lower,
    leaf_upper,
    leaf_front,
):
    tile = l_blocks.shape[-1]
    panel_count = inv_upper.shape[0]
    tiles_side = row_order.shape[0]
    rows_owned = front_in.shape[0]
    cols_owned = front_in.shape[1]
    grid_row = lax.axis_index("row")
    grid_col = lax.axis_index("col")
    col_count = lax.axis_size("col")
    lower_ids = l_ids[0]
    upper_ids = u_ids[0]
    place = grid_row * col_count + grid_col
    my_lower = lower_ids[place]
    my_upper = upper_ids[place]
    inv_u = lax.dynamic_index_in_dim(inv_upper, my_lower % panel_count, 0, keepdims=False)
    inv_l = lax.dynamic_index_in_dim(inv_lower, my_upper // tiles_side, 0, keepdims=False)
    lower = jnp.dot(l_blocks[0, 0], inv_u, preferred_element_type=jnp.float32).astype(jnp.bfloat16)
    upper = jnp.dot(inv_l, u_blocks[0, 0], preferred_element_type=jnp.float32).astype(jnp.bfloat16)
    owned_rows = lax.dynamic_slice_in_dim(row_order, grid_row * rows_owned, rows_owned)
    owned_cols = lax.dynamic_slice_in_dim(col_order, grid_col * cols_owned, cols_owned)
    panel = jnp.arange(panel_count, dtype=jnp.int32)
    want_lower = owned_rows[:, None] * panel_count + panel[None, :]
    want_upper = panel[:, None] * tiles_side + owned_cols[None, :]
    empty_lower = jnp.zeros((rows_owned, panel_count, tile, tile), jnp.bfloat16)
    empty_upper = jnp.zeros((panel_count, cols_owned, tile, tile), jnp.bfloat16)
    low_sel = place_all(
        empty_lower,
        lax.all_gather(lower[None], ("row", "col"), axis=0, tiled=True),
        lower_ids,
        want_lower,
    )
    up_sel = place_all(
        empty_upper,
        lax.all_gather(upper[None], ("row", "col"), axis=0, tiled=True),
        upper_ids,
        want_upper,
    )
    schur = jnp.einsum("pkab,kqbc->pqac", low_sel, up_sel, preferred_element_type=jnp.float32)
    summed = lax.psum_scatter(
        schur.astype(jnp.bfloat16), "layer", scatter_dimension=2, tiled=True
    ).astype(jnp.float32)
    front_out = front_in - summed
    update = jnp.dot(leaf_lower[0], leaf_upper[0], preferred_element_type=jnp.float32)
    leaf_out = (leaf_front[0].astype(jnp.float32) - update).astype(jnp.bfloat16)[None]
    return (front_out, leaf_out)


def solution(mesh):
    return jax.shard_map(
        shards,
        mesh=mesh,
        in_specs=(
            P("layer", ("row", "col"), None, None),
            P("layer", None),
            P("layer", ("row", "col"), None, None),
            P("layer", None),
            P(),
            P(),
            P(),
            P(),
            P("row", "col", "layer", None),
            P(("layer", "row", "col"), None, None),
            P(("layer", "row", "col"), None, None),
            P(("layer", "row", "col"), None, None),
        ),
        out_specs=(P("row", "col", "layer", None), P(("layer", "row", "col"), None, None)),
        check_vma=False,
    )
```

profile of v0, /device:TPU:2, one launch (start us, length us, event | category | flops | bytes accessed | tf_op | source)
XLA Modules:
  0.0 250.7 jit_solution(5410724124969795494)
XLA Ops:
  7.2 0.0 copy-start
  7.2 0.0 all-gather.7.cloned.1.call-start
  7.2 1.4 constant_dynamic-slice_fusion
  10.6 1.9 fusion.29
  12.4 0.0 all-gather.7.cloned.1.call-update
  12.5 0.0 all-gather.5.cloned.1.call-start
  15.1 1.8 convolution_convert_fusion.1
  16.9 0.0 all-gather.5.cloned.1.call-update
  17.0 0.0 all-reduce.3.cloned.1.call-start
  17.0 0.7 dynamic-slice_multiply_fusion
  17.8 0.1 iota_add_fusion
  17.8 1.4 fusion.38
  19.2 0.1 reshape.78
  19.3 0.7 dynamic_slice.19
  20.1 0.1 broadcast_add_fusion
  20.1 1.4 fusion.37
  21.5 0.1 copy.27
  21.6 0.1 reshape.70
  21.7 0.9 compare_reduce_fusion.1
  22.6 0.1 copy.26
  22.7 1.3 dynamic-slice.2
  24.6 0.9 compare_reduce_fusion
  25.5 75.3 %all-gather.7.cloned.1.call-done = bf16[16384,256]{0,1:T(8,128)(2,1)} async-done(((bf16[256,256]{0,1:T(8,128)(2,1)}), bf16[16384,256]{0,1:T(8,128)(2,1)}) %all-gather.7.cloned.1.call-update) | async-done | bytes 8388624 | tf_op jit(solution)/shard_map/all_gather | solution.py:55
  100.8 11.9 %copy.37 = bf16[16384,256]{1,0:T(8,128)(2,1)} copy(bf16[16384,256]{0,1:T(8,128)(2,1)} %all-gather.7.cloned.1.call-done) | data formatting | bytes 16777216 | tf_op jit(solution)/shard_map/all_gather | solution.py:55
  112.7 5.4 %gather_fusion.1 = bf16[16,256,256]{2,1,0:T(8,128)(2,1)} fusion(bf16[64,256,256]{2,1,0:T(8,128)(2,1)} %bitcast.60, s32[1024]{0:T(1024)S(1)} %pad_clamp_fusion), kind=kCustom, calls=%fused_computation.1 | custom fusion | bytes 4194368 | tf_op jit(solution)/shard_map/gather | solution.py:11
  118.1 67.2 %all-gather.5.cloned.1.call-done = bf16[16384,256]{1,0:T(8,128)(2,1)} async-done(((bf16[256,256]{1,0:T(8,128)(2,1)}), bf16[16384,256]{1,0:T(8,128)(2,1)}) %all-gather.5.cloned.1.call-update) | async-done | bytes 8388624 | tf_op jit(solution)/shard_map/all_gather | solution.py:61
  185.4 5.5 %gather_fusion = bf16[16,256,256]{2,1,0:T(8,128)(2,1)} fusion(bf16[64,256,256]{2,1,0:T(8,128)(2,1)} %bitcast.63, s32[1024]{0:T(1024)S(1)} %pad_clamp_fusion.1), kind=kCustom, calls=%fused_computation | custom fusion | bytes 4194368 | tf_op jit(solution)/shard_map/gather | solution.py:11
  190.8 3.7 %fusion.24 = bf16[2,2,256,256]{2,3,0,1:T(8,128)(2,1)S(1)} fusion(bf16[2,8,256,256]{3,2,1,0:T(8,128)(2,1)} %bitcast.61, pred[2,8]{1,0:T(4,128)(4,1)S(1)} %compare_reduce_fusion, bf16[8,2,256,256]{3,2,1,0:T(8,128)(2,1)} %bitcast.62, pred[8,2]{1,0:T(8,128)(4,1)S(1)} %copy.26), kind=kOutput, calls=%fused_computation.16 | convolution fusion | flops 1076101120 | bytes 4718624 | tf_op jit(solution)/shard_map/pkab,kqbc->pqac/dot_general | solution.py:65
  194.5 1.2 copy.30
  195.7 0.0 all-reduce.3.cloned.1.call-update
  195.7 0.0 copy-done
  195.7 0.0 copy-start.1
  195.8 5.9 %fusion.1 = bf16[1,1024,1024]{2,1,0:T(8,128)(2,1)} fusion(bf16[1,1024,1024]{2,1,0:T(8,128)(2,1)} %param.23, bf16[1,1024,1024]{2,1,0:T(8,128)(2,1)S(1)} %copy-done, bf16[1,1024,1024]{2,1,0:T(8,128)(2,1)} %param.21), kind=kOutput, calls=%fused_computation.4 | convolution fusion | flops 2150629376 | bytes 8388608 | tf_op jit(solution)/shard_map/dot_general | solution.py:70
  201.7 40.5 %all-reduce.3.cloned.1.call-done = bf16[2,2,256,256]{3,1,0,2:T(2,128)(2,1)} async-done(((bf16[2,2,256,256]{3,1,0,2:T(2,128)(2,1)}), bf16[2,2,256,256]{3,1,0,2:T(2,128)(2,1)}) %all-reduce.3.cloned.1.call-update) | async-done | bytes 524304
  242.2 0.0 copy-done.1
  242.2 1.2 copy_subtract_fusion
  243.4 0.8 copy.32
  (5 shorter events, 0.0 us)
Async XLA Ops:
  7.2 188.6 %copy-start = (bf16[1,1024,1024]{2,1,0:T(8,128)(2,1)S(1)}, bf16[1,1024,1024]{2,1,0:T(8,128)(2,1)}, u32[]{:S(2)}) copy-start(bf16[1,1024,1024]{2,1,0:T(8,128)(2,1)} %param.22) | copy-start | bytes 6291460
  7.2 93.6 %all-gather.7.cloned.1.call-start = ((), (), s32[]{:S(2)}) async-start(), calls=%async_computation.1 | async-start | bytes 8519680 | tf_op jit(solution)/shard_map/all_gather | solution.py:55
  12.5 172.9 %all-gather.5.cloned.1.call-start = ((), (), s32[]{:S(2)}) async-start(), calls=%async_computation | async-start | bytes 8519680 | tf_op jit(solution)/shard_map/all_gather | solution.py:61
  17.0 225.2 %all-reduce.3.cloned.1.call-start = ((), (), s32[]{:S(2)}) async-start(), calls=%async_computation.2 | async-start | bytes 1048576
  195.7 46.5 %copy-start.1 = (f32[2,2,64,256]{3,2,1,0:T(8,128)S(1)}, f32[2,2,64,256]{3,2,1,0:T(8,128)}, u32[]{:S(2)}) copy-start(f32[2,2,64,256]{3,2,1,0:T(8,128)} %param.20) | copy-start | bytes 786436
Sparse Core Ops, SparseCore 0:
  12.6 88.1 all-gather.6
  103.5 81.7 all-gather.4
  195.8 46.3 all-reduce.2
where the time goes:
time: 251 us
  waiting for transfers between devices  183 us (73%)
  local copies, waits for them, and re-layouts  28.5 us (11%)
  between operations  19 us (8%)
  matrix products  13.3 us (5%)
  other arithmetic  6.61 us (3%)
    all_gather x1, waiting for transfers between devices, shards(): lax.all_gather(lower[None], ('row', 'col'), axis=0, tiled=True)  75.3 us
    all_gather x1, waiting for transfers between devices, shards(): lax.all_gather(upper[None], ('row', 'col'), axis=0, tiled=True)  67.2 us
    unnamed x4, waiting for transfers between devices  40.6 us
    all_gather x1, local copies, waits for them, and re-layouts, shards(): lax.all_gather(lower[None], ('row', 'col'), axis=0, tiled=True)  11.9 us
    gather x2, local copies, waits for them, and re-layouts, place_all(): picked = blocks[position]  10.9 us
    dot_general x1, matrix products, shards(): jnp.dot(leaf_lower[0], leaf_upper[0], preferred_element_type=jnp.float32)  5.92 us
  transfers between devices with their start and end apart: 3, of which 3 were waited for; matrix products, arithmetic and copies ran while one was open for 13% of the time, Pallas kernels for 0%

commit v1 on v0

--- a/solution.py
+++ b/solution.py
@@ -58,7 +58,12 @@
     )
     up_sel = place_all(
         empty_upper,
-        lax.all_gather(upper[None], ("row", "col"), axis=0, tiled=True),
+        jnp.concatenate(
+            lax.all_to_all(
+                jnp.stack([upper[None]] * lax.axis_size(("row", "col"))), ("row", "col"), 0, 0
+            ),
+            axis=0,
+        ),
         upper_ids,
         want_upper,
     )

time: 251 us -> 323 us (1.29)
  waiting for transfers between devices: 183 us -> 243 us
  starting transfers between devices: 0.12 us -> 12.4 us
  other arithmetic: 6.61 us -> 3.34 us
    all_to_all x0 -> x1, waiting for transfers between devices: none -> 200 us  [shards(): lax.all_to_all(jnp.stack([upper[None]] * lax.axis_size(('row', 'col'))),...]
    all_gather x1, waiting for transfers between devices: 75.3 us -> 0.01 us  [shards(): lax.all_gather(lower[None], ('row', 'col'), axis=0, tiled=True)]
    all_gather x1 -> x0, waiting for transfers between devices: 67.2 us -> none  [shards(): lax.all_gather(upper[None], ('row', 'col'), axis=0, tiled=True)]
    all_to_all x0 -> x1, starting transfers between devices: none -> 12.4 us  [shards(): lax.all_to_all(jnp.stack([upper[None]] * lax.axis_size(('row', 'col'))),...]
    another operation x0 -> x1, local copies, waits for them, and re-layouts: none -> 4.23 us  [shards(): jnp.stack([upper[None]] * lax.axis_size(('row', 'col')))]
    unnamed x4 -> x3, waiting for transfers between devices: 40.6 us -> 42.8 us
  transfers between devices with their start and end apart: 3 -> 3, of which waited for: 3 -> 2; matrix products, arithmetic and copies ran while one was open for 13% -> 5% of each run, Pallas kernels for 0% -> 0%
where the time goes in v1:
time: 323 us; the launch traced here: 322 us
  waiting for transfers between devices  243 us (75%)
  local copies, waits for them, and re-layouts  31.3 us (10%)
  between operations  19.4 us (6%)
  matrix products  12.6 us (4%)
  starting transfers between devices  12.4 us (4%)
  other arithmetic  3.34 us (1%)
    all_to_all x1, waiting for transfers between devices, shards(): lax.all_to_all(jnp.stack([upper[None]] * lax.axis_size(('row', 'col'))),...  200 us
    unnamed x3, waiting for transfers between devices  42.8 us
    all_to_all x1, starting transfers between devices, shards(): lax.all_to_all(jnp.stack([upper[None]] * lax.axis_size(('row', 'col'))),...  12.4 us
    all_gather x1, local copies, waits for them, and re-layouts, shards(): lax.all_gather(lower[None], ('row', 'col'), axis=0, tiled=True)  11.9 us
    gather x2, local copies, waits for them, and re-layouts, place_all(): picked = blocks[position]  10.8 us
  transfers between devices with their start and end apart: 3, of which 2 were waited for; matrix products, arithmetic and copies ran while one was open for 5% of the time, Pallas kernels for 0%

profile of v1, /device:TPU:2, one launch (start us, length us, event | category | flops | bytes accessed | tf_op | source)
XLA Modules:
  0.0 322.2 jit_solution(2612672614726233450)
XLA Ops:
  7.2 0.0 copy-start
  7.2 1.4 constant_dynamic-slice_fusion
  11.2 1.2 convolution_convert_fusion.1
  12.4 4.2 %stack.3 = bf16[64,1,256,256]{3,2,1,0:T(8,128)(2,1)} broadcast(bf16[256,256]{1,0:T(8,128)(2,1)S(1)} %convolution_convert_fusion.1), dimensions={2,3} | broadcast | bytes 8519680 | tf_op jit(solution)/shard_map/stack | solution.py:63
  16.6 0.0 copy-start.2
  16.6 0.0 copy-start.5
  16.6 0.0 copy-start.3
  16.6 0.0 copy-start.6
  16.6 0.0 copy-start.4
  16.6 0.0 copy-start.7
  16.6 12.4 %all-to-all-start = ((bf16[64,1,256,256]{3,2,1,0:T(8,128)(2,1)}), bf16[64,1,256,256]{3,2,1,0:T(8,128)(2,1)}, u32[]{:S(2)}, u32[]{:S(2)}) async-start(bf16[64,1,256,256]{3,2,1,0:T(8,128)(2,1)} %stack.3), calls=%async_computation | async-start | bytes 16777216 | tf_op jit(solution)/shard_map/all_to_all | solution.py:62
  29.0 0.0 all-gather.3.cloned.1.call-start
  31.0 0.0 copy-done.2
  31.0 1.8 fusion.29
  32.8 0.0 all-gather.3.cloned.1.call-update
  32.8 0.0 all-reduce.3.cloned.1.call-start
  32.9 0.0 copy-done.5
  32.9 0.1 dynamic_slice.19
  33.0 0.1 broadcast_add_fusion
  33.1 0.0 copy-done.3
  33.1 0.7 fusion.37
  33.8 0.1 copy.27
  33.9 0.1 reshape.76
  34.0 0.0 copy-done.6
  34.0 0.1 dynamic-slice_multiply_fusion
  34.1 0.1 iota_add_fusion
  34.1 0.0 copy-done.4
  34.1 0.8 fusion.38
  34.9 0.1 reshape.84
  35.0 0.2 compare_reduce_fusion.1
  35.2 0.1 copy.26
  35.3 0.0 copy-done.7
  35.3 0.6 dynamic-slice.2
  36.6 0.2 compare_reduce_fusion
  36.8 200.3 %all-to-all-done = bf16[64,1,256,256]{3,2,1,0:T(8,128)(2,1)} async-done(((bf16[64,1,256,256]{3,2,1,0:T(8,128)(2,1)}), bf16[64,1,256,256]{3,2,1,0:T(8,128)(2,1)}, u32[]{:S(2)}, u32[]{:S(2)}) %all-to-all-start) | async-done | bytes 8388640 | tf_op jit(solution)/shard_map/all_to_all | solution.py:62
  237.1 5.4 %gather_fusion = bf16[16,256,256]{2,1,0:T(8,128)(2,1)} fusion(bf16[64,256,256]{2,1,0:T(8,128)(2,1)} %bitcast.4, s32[1024]{0:T(1024)S(1)} %pad_clamp_fusion.1), kind=kCustom, calls=%fused_computation | custom fusion | bytes 4194368 | tf_op jit(solution)/shard_map/gather | solution.py:11
  242.5 0.0 all-gather.3.cloned.1.call-done
  242.5 11.9 %copy.37 = bf16[16384,256]{1,0:T(8,128)(2,1)} copy(bf16[16384,256]{0,1:T(8,128)(2,1)} %all-gather.3.cloned.1.call-done) | data formatting | bytes 16777216 | tf_op jit(solution)/shard_map/all_gather | solution.py:55
  254.3 5.4 %gather_fusion.1 = bf16[16,256,256]{2,1,0:T(8,128)(2,1)} fusion(bf16[64,256,256]{2,1,0:T(8,128)(2,1)} %bitcast.60, s32[1024]{0:T(1024)S(1)} %pad_clamp_fusion), kind=kCustom, calls=%fused_computation.1 | custom fusion | bytes 4194368 | tf_op jit(solution)/shard_map/gather | solution.py:11
  259.7 3.7 %fusion.24 = bf16[2,2,256,256]{2,3,0,1:T(8,128)(2,1)S(1)} fusion(bf16[2,8,256,256]{3,2,1,0:T(8,128)(2,1)} %bitcast.62, pred[2,8]{1,0:T(4,128)(4,1)S(1)} %compare_reduce_fusion, bf16[8,2,256,256]{3,2,1,0:T(8,128)(2,1)} %bitcast.61, pred[8,2]{1,0:T(8,128)(4,1)S(1)} %copy.26), kind=kOutput, calls=%fused_computation.16 | convolution fusion | flops 1076101120 | bytes 4718624 | tf_op jit(solution)/shard_map/pkab,kqbc->pqac/dot_general | solution.py:70
  263.4 1.2 copy.30
  264.6 0.0 all-reduce.3.cloned.1.call-update
  264.6 0.0 copy-done
  264.6 0.0 copy-start.1
  264.7 5.9 %fusion.1 = bf16[1,1024,1024]{2,1,0:T(8,128)(2,1)} fusion(bf16[1,1024,1024]{2,1,0:T(8,128)(2,1)} %param.23, bf16[1,1024,1024]{2,1,0:T(8,128)(2,1)S(1)} %copy-done, bf16[1,1024,1024]{2,1,0:T(8,128)(2,1)} %param.21), kind=kOutput, calls=%fused_computation.4 | convolution fusion | flops 2150629376 | bytes 8388608 | tf_op jit(solution)/shard_map/dot_general | solution.py:75
  270.6 42.8 %all-reduce.3.cloned.1.call-done = bf16[2,2,256,256]{3,1,0,2:T(2,128)(2,1)} async-done(((bf16[2,2,256,256]{3,1,0,2:T(2,128)(2,1)}), bf16[2,2,256,256]{3,1,0,2:T(2,128)(2,1)}) %all-reduce.3.cloned.1.call-update) | async-done | bytes 524304
  313.4 0.0 copy-done.1
  313.4 1.2 copy_subtract_fusion
  314.6 0.8 copy.32
  (5 shorter events, 0.0 us)
Async XLA Ops:
  7.2 257.5 %copy-start = (bf16[1,1024,1024]{2,1,0:T(8,128)(2,1)S(1)}, bf16[1,1024,1024]{2,1,0:T(8,128)(2,1)}, u32[]{:S(2)}) copy-start(bf16[1,1024,1024]{2,1,0:T(8,128)(2,1)} %param.22) | copy-start | bytes 6291460
  16.6 14.4 %copy-start.2 = (bf16[1,1,256,256]{3,2,1,0:T(8,128)(2,1)S(1)}, bf16[1,1,256,256]{3,2,1,0:T(8,128)(2,1)}, u32[]{:S(2)}) copy-start(bf16[1,1,256,256]{3,2,1,0:T(8,128)(2,1)} %param.12) | copy-start | bytes 393220
  16.6 16.3 %copy-start.5 = (s32[16]{0:T(128)S(1)}, s32[16]{0:T(128)}, u32[]{:S(2)}) copy-start(s32[16]{0:T(128)} %param.19) | copy-start | bytes 196
  16.6 16.5 %copy-start.3 = (s32[1,64]{1,0:T(1,128)S(1)}, s32[1,64]{1,0:T(1,128)}, u32[]{:S(2)}) copy-start(s32[1,64]{1,0:T(1,128)} %param.15) | copy-start | bytes 772
  16.6 17.4 %copy-start.6 = (s32[16]{0:T(128)S(1)}, s32[16]{0:T(128)}, u32[]{:S(2)}) copy-start(s32[16]{0:T(128)} %param.18) | copy-start | bytes 196
  16.6 17.5 %copy-start.4 = (s32[1,64]{1,0:T(1,128)S(1)}, s32[1,64]{1,0:T(1,128)}, u32[]{:S(2)}) copy-start(s32[1,64]{1,0:T(1,128)} %param.13) | copy-start | bytes 772
  16.6 18.7 %copy-start.7 = (u32[256]{0:T(256)S(1)}, u32[256]{0:T(256)}, u32[]{:S(2)}) copy-start(u32[256]{0:T(256)} %constant.79) | copy-start | bytes 3076
  16.6 220.4 %all-to-all-start = ((bf16[64,1,256,256]{3,2,1,0:T(8,128)(2,1)}), bf16[64,1,256,256]{3,2,1,0:T(8,128)(2,1)}, u32[]{:S(2)}, u32[]{:S(2)}) async-start(bf16[64,1,256,256]{3,2,1,0:T(8,128)(2,1)} %stack.3), calls=%async_computation | async-start | bytes 16777216 | tf_op jit(solution)/shard_map/all_to_all | solution.py:62
  29.0 213.5 %all-gather.3.cloned.1.call-start = ((), (), s32[]{:S(2)}) async-start(), calls=%async_computation.1 | async-start | bytes 8519680 | tf_op jit(solution)/shard_map/all_gather | solution.py:55
  32.8 280.6 %all-reduce.3.cloned.1.call-start = ((), (), s32[]{:S(2)}) async-start(), calls=%async_computation.2 | async-start | bytes 1048576
  264.6 48.7 %copy-start.1 = (f32[2,2,64,256]{3,2,1,0:T(8,128)S(1)}, f32[2,2,64,256]{3,2,1,0:T(8,128)}, u32[]{:S(2)}) copy-start(f32[2,2,64,256]{3,2,1,0:T(8,128)} %param.20) | copy-start | bytes 786436
Sparse Core Ops, SparseCore 0:
  33.0 181.0 all-gather.2
  264.8 48.5 all-reduce.2
